TPU v7x, 32 devices: a whole 2x2x4 slice. The times are simulated.
32 devices in a mesh: sx: 4 (over z), sy: 4 (over y, x), dp: 2 (over core).
Axes of the slice: x: 2, y: 2, z: 4, core: 2. Of those that a mesh axis runs over, the one named last changes fastest.
Arguments:
- features: bfloat16 [2, 32, 32, 4, 8, 128], P('dp', 'sx', 'sy'), may hold values from -6 to 6
- cotangent: bfloat16 [2, 32, 32, 4, 8, 128], P('dp', 'sx', 'sy'), may hold values from -6 to 6
- first_weight: bfloat16 [27, 128, 128], replicated, may hold values from -0.109375 to 0.109375
- second_weight: bfloat16 [27, 128, 128], replicated, may hold values from -0.109375 to 0.109375
- neighbours: int32 [2, 4, 4, 4, 26], P('dp', 'sx', 'sy'), may hold values from -1 to 3, as said below
- counts: int32 [2, 4, 4], P('dp', 'sx', 'sy'), may hold values from 1 to 4, as said below
Outputs:
- out_field: bfloat16 [2, 32, 32, 4, 8, 128], P('dp', 'sx', 'sy')
- grad_input: bfloat16 [2, 32, 32, 4, 8, 128], P('dp', 'sx', 'sy')
- grad_first: float32 [27, 128, 128], replicated
- grad_second: float32 [27, 128, 128], replicated
Inputs may be any that keep to these rules, and one draw needn't show every extreme that they name: Entries name only live slots; slots at or above a column's count have no neighbours; the relation is symmetric: if slot s of column (i, j) names slot t in direction d, then slot t of column (i+dx, j+dy) names s in the opposite direction, and the blocks are adjacent in space; columns outside the grid are never named. `counts`: some column of every workpiece has 4 live slots.
All inputs are finite; a program needn't handle non-finite values.
Results may differ from a plain program's by a relative error of at most 0.012.
Values may be sent and summed in bfloat16 or wider, within the bound.
A program may use at most 192 MiB of HBM per device.

v0:
```python
import jax
import jax.numpy as jnp
from jax import lax
from jax.sharding import PartitionSpec as P


def with_halo(cells, sides, width):
    for axis, dim in sides:
        count = lax.axis_size(axis)
        ends = count - 1
        head = lax.slice_in_dim(cells, 0, width, axis=dim)
        tail = lax.slice_in_dim(cells, cells.shape[dim] - width, cells.shape[dim], axis=dim)
        cells = jnp.concatenate(
            [
                lax.ppermute(tail, axis, [(i, (i + 1) % count) for i in range(ends)]),
                cells,
                lax.ppermute(head, axis, [((i + 1) % count, i) for i in range(ends)]),
            ],
            axis=dim,
        )
    return cells


def padded_blocks(halo_field, neighbour):
    block_edge = halo_field.shape[0] - 2
    ranges_xy = [(0, 1), (1, block_edge + 1), (block_edge + 1, block_edge + 2)]
    ranges_z = [(block_edge - 1, block_edge), (0, block_edge), (0, 1)]
    planes = []
    for shift_x in range(3):
        row_list = []
        for shift_y in range(3):
            slab_list = []
            for shift_z in range(3):
                direction = shift_x * 9 + shift_y * 3 + shift_z
                low_x, high_x = ranges_xy[shift_x]
                low_y, high_y = ranges_xy[shift_y]
                low_z, high_z = ranges_z[shift_z]
                region = halo_field[low_x:high_x, low_y:high_y, :, low_z:high_z]
                if direction == 13:
                    slab_piece = region
                else:
                    entry = direction if direction < 13 else direction - 1
                    target = neighbour[:, entry]
                    valid = (target >= 0).astype(region.dtype)[None, None, :, None, None]
                    slab_piece = jnp.take(region, jnp.maximum(target, 0), axis=2) * valid
                slab_list.append(slab_piece)
            row_list.append(jnp.concatenate(slab_list, axis=3))
        planes.append(jnp.concatenate(row_list, axis=1))
    return jnp.concatenate(planes, axis=0)


def patch_matrix(padded, block_edge):
    pieces = []
    for shift_x in range(3):
        for shift_y in range(3):
            for shift_z in range(3):
                pieces.append(
                    padded[
                        shift_x : shift_x + block_edge,
                        shift_y : shift_y + block_edge,
                        :,
                        shift_z : shift_z + block_edge,
                    ]
                )
    stacked = jnp.concatenate(pieces, axis=-1)
    return stacked.reshape(-1, stacked.shape[-1])


def flipped_weight(weight):
    return jnp.transpose(weight[::-1], (0, 2, 1))


def silu_slope(values):
    logistic = jax.nn.sigmoid(values)
    return logistic * (1.0 + values * (1.0 - logistic))


def exchanged(values, neighbour):
    halo_field = with_halo(values, (("sx", 0), ("sy", 1)), 1)
    return patch_matrix(padded_blocks(halo_field, neighbour), values.shape[0])


def convolve(columns, weight, shape):
    matrix = weight.reshape(-1, weight.shape[2])
    return jnp.dot(columns, matrix, preferred_element_type=jnp.float32).reshape(shape)


def weight_partial(columns, grads):
    channels = grads.shape[-1]
    term = lax.dot_general(
        columns,
        grads.reshape(-1, channels),
        (((0,), (0,)), ((), ())),
        preferred_element_type=jnp.float32,
    )
    return term.reshape(27, channels, channels)


def sum_gradients(first_part, second_part):
    first_total, second_total = lax.psum((first_part, second_part), ("sx", "sy", "dp"))
    return (first_total, second_total)


def shards(features, cotangent, first_weight, second_weight, neighbours, counts):
    voxels_in = features[0]
    upstream = cotangent[0]
    neighbour = neighbours[0, 0, 0]
    block_edge = voxels_in.shape[0]
    slot_count = voxels_in.shape[2]
    shape = voxels_in.shape
    grad_scale = float(
        lax.axis_size("sx") * lax.axis_size("sy") * lax.axis_size("dp") * slot_count * block_edge**3
    ) ** (-0.5)
    live_mask = (jnp.arange(slot_count, dtype=jnp.int32) < counts[0, 0, 0]).astype(jnp.float32)[
        None, None, :, None, None
    ]
    masked = voxels_in * live_mask.astype(voxels_in.dtype)
    input_columns = exchanged(masked, neighbour)
    pre_first = convolve(input_columns, first_weight, shape)
    hidden = (jax.nn.silu(pre_first) * live_mask).astype(jnp.bfloat16)
    hidden_columns = exchanged(hidden, neighbour)
    pre_second = convolve(hidden_columns, second_weight, shape)
    summed = masked.astype(jnp.float32) + pre_second
    out_block = (jax.nn.silu(summed) * live_mask).astype(jnp.bfloat16)
    back_second = (upstream.astype(jnp.float32) * silu_slope(summed) * live_mask).astype(
        jnp.bfloat16
    )
    second_part = weight_partial(hidden_columns, back_second)
    back_hidden = convolve(exchanged(back_second, neighbour), flipped_weight(second_weight), shape)
    back_first = (back_hidden * silu_slope(pre_first) * live_mask).astype(jnp.bfloat16)
    first_part = weight_partial(input_columns, back_first)
    first_total, second_total = sum_gradients(first_part, second_part)
    back_input = convolve(exchanged(back_first, neighbour), flipped_weight(first_weight), shape)
    input_block = ((back_second.astype(jnp.float32) + back_input) * live_mask).astype(jnp.bfloat16)
    return (out_block[None], input_block[None], first_total * grad_scale, second_total * grad_scale)


def solution(mesh):
    in_specs = (
        P("dp", "sx", "sy", None, None, None),
        P("dp", "sx", "sy", None, None, None),
        P(),
        P(),
        P("dp", "sx", "sy", None, None),
        P("dp", "sx", "sy"),
    )
    out_specs = (
        P("dp", "sx", "sy", None, None, None),
        P("dp", "sx", "sy", None, None, None),
        P(),
        P(),
    )
    return jax.shard_map(shards, mesh=mesh, in_specs=in_specs, out_specs=out_specs, check_vma=False)
```

profile of v0, /device:TPU:0, one launch (start us, length us, event | category | flops | bytes accessed | tf_op | source)
XLA Modules:
  0.0 502.4 jit_solution(4962648479938337616)
XLA Ops:
  11.6 5.6 %collective-permute-start = (bf16[1,8,4,8,128]{4,3,2,1,0:T(8,128)(2,1)S(1)}, bf16[1,8,4,8,128]{4,3,2,1,0:T(8,128)(2,1)S(1)}, u32[]{:S(2)}, u32[]{:S(2)}) collective-permute-start(bf16[1,8,4,8,128]{4,3,2,1,0:T(8,128)(2,1)S(1)} %get-tuple-element.97), channel_id=1, source_target_pairs={{0,8},{8,16},{16,24},{1,9},{9,17},{17,25},{2,10},{10,18},{18,26},{... | collective-permute-start | bytes 196616 | tf_op jit(solution)/shard_map/ppermute | solution.py:15
  17.2 1.9 maximum_reduce_fusion.8
  19.1 2.4 fusion.137
  29.8 1.8 fusion.139
  58.4 4.7 collective-permute-start.2
  85.4 1.6 maximum_maximum_fusion.9
  87.0 2.2 maximum_maximum_fusion
  112.2 3.2 maximum_maximum_fusion.1
  124.6 8.5 %multiply_convert_fusion.1 = (bf16[8,8,4,8,128]{4,3,2,1,0:T(8,128)(2,1)S(1)}, f32[8,8,4,8,128]{4,3,2,1,0:T(8,128)}) fusion(f32[4]{0:T(128)S(1)} %copy-done.57, bf16[8,8,4,8,3456]{4,3,2,1,0:T(8,128)(2,1)} %slice_dynamic-update-slice_fusion.72, bf16[3456,128,1,1,1]{1,0,4,3,2:T(8,128)(2,1)S(1)} %bitcast.657), kind=kOutput, calls=%fused_computation.133 | convolution fusion | flops 1813512192 | bytes 16613392 | tf_op jit(solution)/shard_map/dot_general | solution.py:85
  134.6 4.6 collective-permute-start.4
  141.2 17.9 %copy.150 = bf16[3456,2048]{1,0:T(8,128)(2,1)} copy(bf16[3456,2048]{0,1:T(8,128)(2,1)} %bitcast.253) | data formatting | bytes 28311552 | tf_op jit(solution)/shard_map/dot_general | solution.py:90
  160.6 5.4 %collective-permute-start.6 = (bf16[10,1,4,8,128]{4,3,2,1,0:T(8,128)(2,1)S(1)}, bf16[10,1,4,8,128]{4,3,2,1,0:T(8,128)(2,1)S(1)}, u32[]{:S(2)}, u32[]{:S(2)}) collective-permute-start(bf16[10,1,4,8,128]{4,3,2,1,0:T(8,128)(2,1)S(1)} %get-tuple-element.79), channel_id=1, source_target_pairs={{0,2},{2,4},{4,6},{1,3},{3,5},{5,7},{8,10},{10,12},{12,14},{9,11},... | collective-permute-start | bytes 245768 | tf_op jit(solution)/shard_map/ppermute | solution.py:15
  180.5 2.0 maximum_maximum_fusion.11
  182.5 2.2 maximum_maximum_fusion.2
  207.4 3.2 maximum_maximum_fusion.3
  219.8 10.1 %fusion.6 = (bf16[8,8,4,8,128]{4,3,2,1,0:T(8,128)(2,1)S(1)}, bf16[1,8,8,4,8,128]{5,4,3,2,1,0:T(8,128)(2,1)}) fusion(bf16[1,8,8,4,8,128]{5,4,3,2,1,0:T(8,128)(2,1)S(1)} %copy-done.60, f32[4]{0:T(128)S(1)} %copy-done.57, bf16[8,8,4,8,3456]{4,3,2,1,0:T(8,128)(2,1)} %slice_dynamic-update-slice_fusion.48, bf16[3456,128,1,1,1]{1,0,4,3,2:T(8,128)(2,1)S(1)} %bitcast.658, ...), kind=kOutput, calls=%fused_computation.130 | convolution fusion | flops 1816133632 | bytes 17137680 | tf_op jit(solution)/shard_map/dot_general | solution.py:85
  231.6 4.5 collective-permute-start.8
  237.8 18.8 %copy.151 = bf16[3456,2048]{1,0:T(8,128)(2,1)} copy(bf16[3456,2048]{0,1:T(8,128)(2,1)} %bitcast.258) | data formatting | bytes 28311552 | tf_op jit(solution)/shard_map/dot_general | solution.py:90
  256.5 8.2 %fusion.180 = f32[27,128,128]{2,1,0:T(8,128)} fusion(bf16[27,128,2048]{2,1,0:T(8,128)(2,1)} %bitcast.651, bf16[2048,128,1]{1,0,2:T(8,128)(2,1)S(1)} %bitcast.648), kind=kOutput, calls=%fused_computation.762 | convolution fusion | flops 1811939328 | bytes 16449536 | tf_op jit(solution)/shard_map/dot_general | solution.py:90
  266.3 5.4 %collective-permute-start.10 = (bf16[10,1,4,8,128]{4,3,2,1,0:T(8,128)(2,1)S(1)}, bf16[10,1,4,8,128]{4,3,2,1,0:T(8,128)(2,1)S(1)}, u32[]{:S(2)}, u32[]{:S(2)}) collective-permute-start(bf16[10,1,4,8,128]{4,3,2,1,0:T(8,128)(2,1)S(1)} %get-tuple-element.77), channel_id=1, source_target_pairs={{0,2},{2,4},{4,6},{1,3},{3,5},{5,7},{8,10},{10,12},{12,14},{9,11},... | collective-permute-start | bytes 245768 | tf_op jit(solution)/shard_map/ppermute | solution.py:15
  287.7 2.2 maximum_maximum_fusion.4
  312.6 3.2 maximum_maximum_fusion.5
  325.0 9.1 %fusion.3 = bf16[8,8,4,8,128]{4,3,2,1,0:T(8,128)(2,1)S(1)} fusion(bf16[8,8,4,8,3456]{4,3,2,1,0:T(8,128)(2,1)} %slice_dynamic-update-slice_fusion.24, bf16[3456,128,1,1,1]{1,0,4,3,2:T(8,128)(2,1)S(1)} %bitcast.659, f32[8,8,4,8,128]{4,3,2,1,0:T(8,128)S(1)} %copy-done.61, f32[4]{0:T(128)S(1)} %copy-done.57), kind=kOutput, calls=%fused_computation.118 | convolution fusion | flops 1814560768 | bytes 16613392 | tf_op jit(solution)/shard_map/dot_general | solution.py:85
  335.6 4.8 collective-permute-start.12
  342.0 8.3 %fusion.179 = f32[27,128,128]{2,1,0:T(8,128)} fusion(bf16[27,128,2048]{2,1,0:T(8,128)(2,1)} %bitcast.650, bf16[2048,128,1]{1,0,2:T(8,128)(2,1)S(1)} %bitcast.649), kind=kOutput, calls=%fused_computation.761 | convolution fusion | flops 1811939328 | bytes 16449536 | tf_op jit(solution)/shard_map/dot_general | solution.py:90
  351.8 5.4 %collective-permute-start.14 = (bf16[10,1,4,8,128]{4,3,2,1,0:T(8,128)(2,1)S(1)}, bf16[10,1,4,8,128]{4,3,2,1,0:T(8,128)(2,1)S(1)}, u32[]{:S(2)}, u32[]{:S(2)}) collective-permute-start(bf16[10,1,4,8,128]{4,3,2,1,0:T(8,128)(2,1)S(1)} %get-tuple-element.75), channel_id=1, source_target_pairs={{0,2},{2,4},{4,6},{1,3},{3,5},{5,7},{8,10},{10,12},{12,14},{9,11},... | collective-permute-start | bytes 245768 | tf_op jit(solution)/shard_map/ppermute | solution.py:15
  371.6 1.6 maximum_maximum_fusion.15
  373.2 2.2 maximum_maximum_fusion.6
  398.1 3.2 maximum_maximum_fusion.7
  410.3 8.2 %fusion.4 = bf16[1,8,8,4,8,128]{5,4,3,2,1,0:T(8,128)(2,1)} fusion(bf16[8,8,4,8,3456]{4,3,2,1,0:T(8,128)(2,1)} %slice_dynamic-update-slice_fusion, bf16[3456,128,1,1,1]{1,0,4,3,2:T(8,128)(2,1)S(1)} %bitcast.656, bf16[8,8,4,8,128]{4,3,2,1,0:T(8,128)(2,1)S(1)} %get-tuple-element.65, f32[4]{0:T(128)S(1)} %copy-done.57), kind=kOutput, calls=%fused_computation.119 | convolution fusion | flops 1812987904 | bytes 16089104 | tf_op jit(solution)/shard_map/dot_general | solution.py:85
  418.6 72.3 %all-reduce.3.cloned.1.call-done = (f32[27,128,128]{2,1,0:T(8,128)}, f32[27,128,128]{2,1,0:T(8,128)}) async-done(((f32[27,128,128]{2,1,0:T(8,128)}, f32[27,128,128]{2,1,0:T(8,128)}), (f32[27,128,128]{2,1,0:T(8,128)}, f32[27,128,128]{2,1,0:T(8,128)})) %all-reduce.3.cloned.1.call-update) | async-done | bytes 3538960 | tf_op jit(solution)/shard_map/psum | solution.py:100
  490.9 3.0 broadcast_multiply_fusion.1
  (653 shorter events, 247.3 us)
Async XLA Ops:
  7.2 40.9 %copy-start.3 = (bf16[27,128,128]{2,1,0:T(8,128)(2,1)S(1)}, bf16[27,128,128]{2,1,0:T(8,128)(2,1)}, u32[]{:S(2)}) copy-start(bf16[27,128,128]{2,1,0:T(8,128)(2,1)} %param.23) | copy-start | bytes 2654212
  7.2 483.7 %all-reduce.3.cloned.1.call-start = ((), (), s32[]{:S(2)}) async-start(), calls=%async_computation | async-start | bytes 7077888 | tf_op jit(solution)/shard_map/psum | solution.py:100
  8.5 41.9 %copy-start.2 = (bf16[27,128,128]{2,1,0:T(8,128)(2,1)S(1)}, bf16[27,128,128]{2,1,0:T(8,128)(2,1)}, u32[]{:S(2)}) copy-start(bf16[27,128,128]{2,1,0:T(8,128)(2,1)} %param.22) | copy-start | bytes 2654212
  10.3 46.7 %collective-permute-start.1 = (bf16[1,8,4,8,128]{4,3,2,1,0:T(8,128)(2,1)}, bf16[1,8,4,8,128]{4,3,2,1,0:T(8,128)(2,1)S(1)}, u32[]{:S(2)}, u32[]{:S(2)}) collective-permute-start(bf16[1,8,4,8,128]{4,3,2,1,0:T(8,128)(2,1)} %get-tuple-element.98), channel_id=1, source_target_pairs={{8,0},{16,8},{24,16},{9,1},{17,9},{25,17},{10,2},{18,10},{26,18},{... | collective-permute-start | bytes 196616 | tf_op jit(solution)/shard_map/ppermute | solution.py:17
  11.6 45.4 %collective-permute-start = (bf16[1,8,4,8,128]{4,3,2,1,0:T(8,128)(2,1)S(1)}, bf16[1,8,4,8,128]{4,3,2,1,0:T(8,128)(2,1)S(1)}, u32[]{:S(2)}, u32[]{:S(2)}) collective-permute-start(bf16[1,8,4,8,128]{4,3,2,1,0:T(8,128)(2,1)S(1)} %get-tuple-element.97), channel_id=1, source_target_pairs={{0,8},{8,16},{16,24},{1,9},{9,17},{17,25},{2,10},{10,18},{18,26},{... | collective-permute-start | bytes 196616 | tf_op jit(solution)/shard_map/ppermute | solution.py:15
  54.0 33.0 %copy-start.51 = (s32[1024]{0:T(1024)}, s32[1024]{0:T(1024)S(1)}, u32[]{:S(2)}) copy-start(s32[1024]{0:T(1024)S(1)} %get-tuple-element.219) | copy-start | bytes 12292
  54.7 32.3 %copy-start.52 = (s32[1024]{0:T(1024)}, s32[1024]{0:T(1024)S(1)}, u32[]{:S(2)}) copy-start(s32[1024]{0:T(1024)S(1)} %get-tuple-element.222) | copy-start | bytes 12292
  54.7 32.3 %copy-start.53 = (s32[1024]{0:T(1024)}, s32[1024]{0:T(1024)S(1)}, u32[]{:S(2)}) copy-start(s32[1024]{0:T(1024)S(1)} %get-tuple-element.221) | copy-start | bytes 12292
  55.4 31.6 %copy-start.48 = (s32[1024]{0:T(1024)}, s32[1024]{0:T(1024)S(1)}, u32[]{:S(2)}) copy-start(s32[1024]{0:T(1024)S(1)} %get-tuple-element.224) | copy-start | bytes 12292
  57.1 13.1 %collective-permute-start.3 = (bf16[10,1,4,8,128]{4,3,2,1,0:T(8,128)(2,1)S(1)}, bf16[10,1,4,8,128]{4,3,2,1,0:T(8,128)(2,1)S(1)}, u32[]{:S(2)}, u32[]{:S(2)}) collective-permute-start(bf16[10,1,4,8,128]{4,3,2,1,0:T(8,128)(2,1)S(1)} %get-tuple-element.82), channel_id=1, source_target_pairs={{2,0},{4,2},{6,4},{3,1},{5,3},{7,5},{10,8},{12,10},{14,12},{11,9},... | collective-permute-start | bytes 245768 | tf_op jit(solution)/shard_map/ppermute | solution.py:17
  58.4 11.9 %collective-permute-start.2 = (bf16[10,1,4,8,128]{4,3,2,1,0:T(8,128)(2,1)S(1)}, bf16[10,1,4,8,128]{4,3,2,1,0:T(8,128)(2,1)S(1)}, u32[]{:S(2)}, u32[]{:S(2)}) collective-permute-start(bf16[10,1,4,8,128]{4,3,2,1,0:T(8,128)(2,1)S(1)} %get-tuple-element.81), channel_id=1, source_target_pairs={{0,2},{2,4},{4,6},{1,3},{3,5},{5,7},{8,10},{10,12},{12,14},{9,11},... | collective-permute-start | bytes 245768 | tf_op jit(solution)/shard_map/ppermute | solution.py:15
  133.3 25.9 %collective-permute-start.5 = (bf16[1,8,4,8,128]{4,3,2,1,0:T(8,128)(2,1)S(1)}, bf16[1,8,4,8,128]{4,3,2,1,0:T(8,128)(2,1)S(1)}, u32[]{:S(2)}, u32[]{:S(2)}) collective-permute-start(bf16[1,8,4,8,128]{4,3,2,1,0:T(8,128)(2,1)S(1)} %get-tuple-element.94), channel_id=1, source_target_pairs={{8,0},{16,8},{24,16},{9,1},{17,9},{25,17},{10,2},{18,10},{26,18},{... | collective-permute-start | bytes 196616 | tf_op jit(solution)/shard_map/ppermute | solution.py:17
  134.6 24.6 %collective-permute-start.4 = (bf16[1,8,4,8,128]{4,3,2,1,0:T(8,128)(2,1)S(1)}, bf16[1,8,4,8,128]{4,3,2,1,0:T(8,128)(2,1)S(1)}, u32[]{:S(2)}, u32[]{:S(2)}) collective-permute-start(bf16[1,8,4,8,128]{4,3,2,1,0:T(8,128)(2,1)S(1)} %get-tuple-element.93), channel_id=1, source_target_pairs={{0,8},{8,16},{16,24},{1,9},{9,17},{17,25},{2,10},{10,18},{18,26},{... | collective-permute-start | bytes 196616 | tf_op jit(solution)/shard_map/ppermute | solution.py:15
  141.1 28.0 %copy-start.23 = (bf16[4]{0:T(256)(128)(2,1)S(1)}, bf16[4]{0:T(256)(128)(2,1)}, u32[]{:S(2)}) copy-start(bf16[4]{0:T(256)(128)(2,1)} %get-tuple-element.52) | copy-start | bytes 28
  141.1 29.6 %copy-start.22 = (bf16[4]{0:T(256)(128)(2,1)S(1)}, bf16[4]{0:T(256)(128)(2,1)}, u32[]{:S(2)}) copy-start(bf16[4]{0:T(256)(128)(2,1)} %get-tuple-element.50) | copy-start | bytes 28
  141.1 29.6 %copy-start.34 = (pred[4]{0:T(512)(128)(4,1)S(1)}, pred[4]{0:T(512)(128)(4,1)}, u32[]{:S(2)}) copy-start(pred[4]{0:T(512)(128)(4,1)} %get-tuple-element.206) | copy-start | bytes 16
  141.1 30.4 %copy-start.13 = (bf16[4]{0:T(256)(128)(2,1)S(1)}, bf16[4]{0:T(256)(128)(2,1)}, u32[]{:S(2)}) copy-start(bf16[4]{0:T(256)(128)(2,1)} %get-tuple-element.28) | copy-start | bytes 28
  141.1 30.4 %copy-start.33 = (pred[4]{0:T(512)(128)(4,1)S(1)}, pred[4]{0:T(512)(128)(4,1)}, u32[]{:S(2)}) copy-start(pred[4]{0:T(512)(128)(4,1)} %get-tuple-element.209) | copy-start | bytes 16
  141.1 32.0 %copy-start.11 = (bf16[4]{0:T(256)(128)(2,1)S(1)}, bf16[4]{0:T(256)(128)(2,1)}, u32[]{:S(2)}) copy-start(bf16[4]{0:T(256)(128)(2,1)} %get-tuple-element.26) | copy-start | bytes 28
  141.2 32.0 %copy-start.30 = (pred[4]{0:T(512)(128)(4,1)S(1)}, pred[4]{0:T(512)(128)(4,1)}, u32[]{:S(2)}) copy-start(pred[4]{0:T(512)(128)(4,1)} %get-tuple-element.211) | copy-start | bytes 16
  141.2 32.9 %copy-start.10 = (bf16[4]{0:T(256)(128)(2,1)S(1)}, bf16[4]{0:T(256)(128)(2,1)}, u32[]{:S(2)}) copy-start(bf16[4]{0:T(256)(128)(2,1)} %get-tuple-element.23) | copy-start | bytes 28
  141.2 32.9 %copy-start.28 = (pred[4]{0:T(512)(128)(4,1)S(1)}, pred[4]{0:T(512)(128)(4,1)}, u32[]{:S(2)}) copy-start(pred[4]{0:T(512)(128)(4,1)} %get-tuple-element.214) | copy-start | bytes 16
  159.3 11.5 %collective-permute-start.7 = (bf16[10,1,4,8,128]{4,3,2,1,0:T(8,128)(2,1)S(1)}, bf16[10,1,4,8,128]{4,3,2,1,0:T(8,128)(2,1)S(1)}, u32[]{:S(2)}, u32[]{:S(2)}) collective-permute-start(bf16[10,1,4,8,128]{4,3,2,1,0:T(8,128)(2,1)S(1)} %get-tuple-element.80), channel_id=1, source_target_pairs={{2,0},{4,2},{6,4},{3,1},{5,3},{7,5},{10,8},{12,10},{14,12},{11,9},... | collective-permute-start | bytes 245768 | tf_op jit(solution)/shard_map/ppermute | solution.py:17
  160.6 12.7 %collective-permute-start.6 = (bf16[10,1,4,8,128]{4,3,2,1,0:T(8,128)(2,1)S(1)}, bf16[10,1,4,8,128]{4,3,2,1,0:T(8,128)(2,1)S(1)}, u32[]{:S(2)}, u32[]{:S(2)}) collective-permute-start(bf16[10,1,4,8,128]{4,3,2,1,0:T(8,128)(2,1)S(1)} %get-tuple-element.79), channel_id=1, source_target_pairs={{0,2},{2,4},{4,6},{1,3},{3,5},{5,7},{8,10},{10,12},{12,14},{9,11},... | collective-permute-start | bytes 245768 | tf_op jit(solution)/shard_map/ppermute | solution.py:15
  230.1 34.9 %collective-permute-start.9 = (bf16[1,8,4,8,128]{4,3,2,1,0:T(8,128)(2,1)S(1)}, bf16[1,8,4,8,128]{4,3,2,1,0:T(8,128)(2,1)S(1)}, u32[]{:S(2)}, u32[]{:S(2)}) collective-permute-start(bf16[1,8,4,8,128]{4,3,2,1,0:T(8,128)(2,1)S(1)} %get-tuple-element.90), channel_id=1, source_target_pairs={{8,0},{16,8},{24,16},{9,1},{17,9},{25,17},{10,2},{18,10},{26,18},{... | collective-permute-start | bytes 196616 | tf_op jit(solution)/shard_map/ppermute | solution.py:17
  231.6 33.4 %collective-permute-start.8 = (bf16[1,8,4,8,128]{4,3,2,1,0:T(8,128)(2,1)S(1)}, bf16[1,8,4,8,128]{4,3,2,1,0:T(8,128)(2,1)S(1)}, u32[]{:S(2)}, u32[]{:S(2)}) collective-permute-start(bf16[1,8,4,8,128]{4,3,2,1,0:T(8,128)(2,1)S(1)} %get-tuple-element.89), channel_id=1, source_target_pairs={{0,8},{8,16},{16,24},{1,9},{9,17},{17,25},{2,10},{10,18},{18,26},{... | collective-permute-start | bytes 196616 | tf_op jit(solution)/shard_map/ppermute | solution.py:15
  265.0 11.6 %collective-permute-start.11 = (bf16[10,1,4,8,128]{4,3,2,1,0:T(8,128)(2,1)S(1)}, bf16[10,1,4,8,128]{4,3,2,1,0:T(8,128)(2,1)S(1)}, u32[]{:S(2)}, u32[]{:S(2)}) collective-permute-start(bf16[10,1,4,8,128]{4,3,2,1,0:T(8,128)(2,1)S(1)} %get-tuple-element.78), channel_id=1, source_target_pairs={{2,0},{4,2},{6,4},{3,1},{5,3},{7,5},{10,8},{12,10},{14,12},{11,9},... | collective-permute-start | bytes 245768 | tf_op jit(solution)/shard_map/ppermute | solution.py:17
  266.3 12.7 %collective-permute-start.10 = (bf16[10,1,4,8,128]{4,3,2,1,0:T(8,128)(2,1)S(1)}, bf16[10,1,4,8,128]{4,3,2,1,0:T(8,128)(2,1)S(1)}, u32[]{:S(2)}, u32[]{:S(2)}) collective-permute-start(bf16[10,1,4,8,128]{4,3,2,1,0:T(8,128)(2,1)S(1)} %get-tuple-element.77), channel_id=1, source_target_pairs={{0,2},{2,4},{4,6},{1,3},{3,5},{5,7},{8,10},{10,12},{12,14},{9,11},... | collective-permute-start | bytes 245768 | tf_op jit(solution)/shard_map/ppermute | solution.py:15
  334.3 16.2 %collective-permute-start.13 = (bf16[1,8,4,8,128]{4,3,2,1,0:T(8,128)(2,1)S(1)}, bf16[1,8,4,8,128]{4,3,2,1,0:T(8,128)(2,1)S(1)}, u32[]{:S(2)}, u32[]{:S(2)}) collective-permute-start(bf16[1,8,4,8,128]{4,3,2,1,0:T(8,128)(2,1)S(1)} %get-tuple-element.86), channel_id=1, source_target_pairs={{8,0},{16,8},{24,16},{9,1},{17,9},{25,17},{10,2},{18,10},{26,18},{... | collective-permute-start | bytes 196616 | tf_op jit(solution)/shard_map/ppermute | solution.py:17
  335.6 14.9 %collective-permute-start.12 = (bf16[1,8,4,8,128]{4,3,2,1,0:T(8,128)(2,1)S(1)}, bf16[1,8,4,8,128]{4,3,2,1,0:T(8,128)(2,1)S(1)}, u32[]{:S(2)}, u32[]{:S(2)}) collective-permute-start(bf16[1,8,4,8,128]{4,3,2,1,0:T(8,128)(2,1)S(1)} %get-tuple-element.85), channel_id=1, source_target_pairs={{0,8},{8,16},{16,24},{1,9},{9,17},{17,25},{2,10},{10,18},{18,26},{... | collective-permute-start | bytes 196616 | tf_op jit(solution)/shard_map/ppermute | solution.py:15
  350.5 11.6 %collective-permute-start.15 = (bf16[10,1,4,8,128]{4,3,2,1,0:T(8,128)(2,1)S(1)}, bf16[10,1,4,8,128]{4,3,2,1,0:T(8,128)(2,1)S(1)}, u32[]{:S(2)}, u32[]{:S(2)}) collective-permute-start(bf16[10,1,4,8,128]{4,3,2,1,0:T(8,128)(2,1)S(1)} %get-tuple-element.76), channel_id=1, source_target_pairs={{2,0},{4,2},{6,4},{3,1},{5,3},{7,5},{10,8},{12,10},{14,12},{11,9},... | collective-permute-start | bytes 245768 | tf_op jit(solution)/shard_map/ppermute | solution.py:17
  351.8 12.7 %collective-permute-start.14 = (bf16[10,1,4,8,128]{4,3,2,1,0:T(8,128)(2,1)S(1)}, bf16[10,1,4,8,128]{4,3,2,1,0:T(8,128)(2,1)S(1)}, u32[]{:S(2)}, u32[]{:S(2)}) collective-permute-start(bf16[10,1,4,8,128]{4,3,2,1,0:T(8,128)(2,1)S(1)} %get-tuple-element.75), channel_id=1, source_target_pairs={{0,2},{2,4},{4,6},{1,3},{3,5},{5,7},{8,10},{10,12},{12,14},{9,11},... | collective-permute-start | bytes 245768 | tf_op jit(solution)/shard_map/ppermute | solution.py:15
  (47 other events, 678.7 us)
Sparse Core Ops, SparseCore 0:
  350.6 140.2 all-reduce.2
where the time goes:
time: 508 us; the launch traced here: 502 us
  local copies, waits for them, and re-layouts  213 us (42%)
  other arithmetic  96.7 us (19%)
  waiting for transfers between devices  72.4 us (14%)
  matrix products  52.4 us (10%)
  starting transfers between devices  51 us (10%)
  between operations  17.3 us (3%)
    unnamed x253, local copies, waits for them, and re-layouts  97.8 us
    psum x1, waiting for transfers between devices, sum_gradients(): lax.psum((first_part, second_part), ('sx', 'sy', 'dp'))  72.3 us
    gather x104, local copies, waits for them, and re-layouts, padded_blocks(): slab_piece = jnp.take(region, jnp.maximum(target, 0), axis=2) * valid  70.7 us
    ppermute x8, starting transfers between devices, with_halo(): lax.ppermute(tail, axis, [(i, (i + 1) % count) for i in range(ends)])  40.4 us
    dot_general x2, local copies, waits for them, and re-layouts, weight_partial(): lax.dot_general(columns, grads.reshape(-1, channels), (((0,), (0,)), ((),...  36.7 us
    dot_general x4, matrix products, convolve(): jnp.dot(columns, matrix, preferred_element_type=jnp.float32).reshape(shape)  35.9 us
    concatenate x8, other arithmetic, padded_blocks(): return jnp.concatenate(planes, axis=0)  21.7 us
    mul x104, other arithmetic, padded_blocks(): slab_piece = jnp.take(region, jnp.maximum(target, 0), axis=2) * valid  18.3 us
  transfers between devices with their start and end apart: 17, of which 1 were waited for; matrix products, arithmetic and copies ran while one was open for 36% of the time, Pallas kernels for 0%

commit v1 on v0

v1 whole, which is shorter than its diff:
```python
import functools

import jax
import jax.numpy as jnp
from jax import lax
from jax.experimental import pallas as pl
from jax.experimental.pallas import tpu as pltpu
from jax.sharding import PartitionSpec as P

DIRS = [(dx, dy) for dx in (-1, 0, 1) for dy in (-1, 0, 1) if (dx, dy) != (0, 0)]
F32 = jnp.float32
BF16 = jnp.bfloat16


def slope(v):
    s = jax.nn.sigmoid(v)
    return s * (1.0 + v * (1.0 - s))


def kernel(
    nx,
    ny,
    feat,
    cot,
    w1,
    w2,
    w1f,
    w2f,
    sel,
    live,
    out_ref,
    gin_ref,
    gw1_ref,
    gw2_ref,
    fld,
    rx,
    ry,
    rc,
    pc_a,
    pc_b,
    pc_c,
    pre,
    gt,
    send_sem,
    recv_sem,
):
    edge = feat.shape[0]
    rows = feat.shape[2]
    ch = feat.shape[3]
    pairs = edge // 2
    plane = edge * rows
    ix = lax.axis_index("sx")
    iy = lax.axis_index("sy")

    def there(dx, dy):
        ok = None
        for d, i, n in ((dx, ix, nx), (dy, iy, ny)):
            if d == 0:
                continue
            c = (i < n - 1) if d > 0 else (i > 0)
            ok = c if ok is None else jnp.logical_and(ok, c)
        return ok

    def peer(dx, dy):
        px = jnp.minimum(jnp.maximum(ix + dx, 0), nx - 1)
        py = jnp.minimum(jnp.maximum(iy + dy, 0), ny - 1)
        return {"sx": px, "sy": py}

    def halo_ref(f, dx, dy):
        if dy == 0:
            return rx.at[f, (dx + 1) // 2]
        if dx == 0:
            return ry.at[f, (dy + 1) // 2]
        return rc.at[f, (dx + 1) // 2 * 2 + (dy + 1) // 2]

    def desc(f, k):
        dx, dy = DIRS[k]
        far_x = edge - 1 if dx > 0 else 0
        far_y = edge - 1 if dy > 0 else 0
        if dy == 0:
            src = fld.at[f, far_x]
        elif dx == 0:
            src = fld.at[f, :, far_y]
        else:
            src = fld.at[f, far_x, far_y]
        return pltpu.make_async_remote_copy(
            src_ref=src,
            dst_ref=halo_ref(f, -dx, -dy),
            send_sem=send_sem.at[f, k],
            recv_sem=recv_sem.at[f, k],
            device_id=peer(dx, dy),
            device_id_type=pl.DeviceIdType.MESH,
        )

    def send(f):
        for k, (dx, dy) in enumerate(DIRS):
            @pl.when(there(dx, dy))
            def _(k=k):
                desc(f, k).start()

    def arrive(f):
        for k, (dx, dy) in enumerate(DIRS):
            @pl.when(there(-dx, -dy))
            def _(k=k):
                desc(f, k).wait_recv()

    def drain(f):
        for k, (dx, dy) in enumerate(DIRS):
            @pl.when(there(dx, dy))
            def _(k=k):
                desc(f, k).wait_send()

    def put(pc, x, yp, tile):
        t = tile.astype(BF16)
        for b in range(3):
            y = yp - b
            if 0 <= y < edge:
                for c in range(3):
                    lo = (b * 3 + c) * ch
                    pc[x, y, :, lo : lo + ch] = t[c * rows : (c + 1) * rows]

    def line(pc, x, s, tiles):
        cat = jnp.concatenate(tiles, axis=1)
        got = jnp.dot(s, cat, preferred_element_type=F32)
        for y in range(edge):
            put(pc, x, y + 1, got[:, y * ch : (y + 1) * ch])

    def inner(f, pc):
        def body(x, carry):
            line(pc, x + 1, sel[4], [fld[f, x, y] for y in range(edge)])
            return carry

        lax.fori_loop(0, edge, body, 0)

    def outer(f, pc):
        for h in range(2):
            x = 0 if h == 0 else edge + 1
            line(pc, x, sel[6 * h + 1], [rx[f, h, y] for y in range(edge)])
            for g in range(2):
                yp = 0 if g == 0 else edge + 1
                put(pc, x, yp, jnp.dot(sel[6 * h + 2 * g], rc[f, h * 2 + g], preferred_element_type=F32))
            cat = jnp.concatenate([ry[f, h, x] for x in range(edge)], axis=1)
            got = jnp.dot(sel[3 + 2 * h], cat, preferred_element_type=F32)
            for x in range(edge):
                put(pc, x + 1, 0 if h == 0 else edge + 1, got[:, x * ch : (x + 1) * ch])

    def conv(pc, w, use):
        def body(i, carry):
            left = None
            right = None
            for p in range(4):
                lhs = pc[2 * i + p].reshape(plane, 9 * ch)
                wl = w[p] if p < 3 else None
                wr = w[p - 1] if p > 0 else None
                if wr is None:
                    left = jnp.dot(lhs, wl, preferred_element_type=F32)
                elif wl is None:
                    right = right + jnp.dot(lhs, wr, preferred_element_type=F32)
                else:
                    both = jnp.dot(lhs, jnp.concatenate([wl, wr], axis=1), preferred_element_type=F32)
                    left = left + both[:, :ch]
                    right = both[:, ch:] if right is None else right + both[:, ch:]
            use(i, 0, left)
            use(i, 1, right)
            return carry

        lax.fori_loop(0, pairs, body, 0)

    def keep_t(i, h, v):
        gt[h * ch : (h + 1) * ch, pl.ds(pl.multiple_of(i * plane, plane), plane)] = v.T.astype(BF16)

    def wgrad(pc, gw):
        def body(b, carry):
            for p in range(4):
                lanes = pl.ds(pl.multiple_of(b * (3 * ch), 3 * ch), 3 * ch)
                acc = None
                for i in range(pairs):
                    rhs = pc[2 * i + p, :, :, lanes].reshape(plane, 3 * ch)
                    lhs = gt[:, i * plane : (i + 1) * plane]
                    if p == 0:
                        lhs = lhs[:ch]
                    elif p == 3:
                        lhs = lhs[ch:]
                    t = jnp.dot(lhs, rhs, preferred_element_type=F32)
                    acc = t if acc is None else acc + t
                if p == 0:
                    gw[0, b] = acc
                elif p == 3:
                    gw[2, b] = gw[2, b] + acc
                else:
                    gw[p - 1, b] = gw[p - 1, b] + acc[ch:]
                    gw[p, b] = acc[:ch]
            return carry

        lax.fori_loop(0, 3, body, 0)

    for dx, dy in DIRS:
        @pl.when(jnp.logical_not(there(dx, dy)))
        def _(dx=dx, dy=dy):
            for f in range(4):
                r = halo_ref(f, dx, dy)
                r[...] = jnp.zeros(r.shape, BF16)

    barrier = pltpu.get_barrier_semaphore()
    for dx, dy in DIRS:
        @pl.when(there(dx, dy))
        def _(dx=dx, dy=dy):
            pl.semaphore_signal(barrier, inc=1, device_id=peer(dx, dy), device_id_type=pl.DeviceIdType.MESH)

    def mask_in(x, carry):
        v = feat[x].astype(F32).reshape(plane, ch) * live[...]
        fld[0, x] = v.astype(BF16).reshape(edge, rows, ch)
        return carry

    lax.fori_loop(0, edge, mask_in, 0)

    near_x = jnp.minimum(ix, 1) + jnp.minimum(nx - 1 - ix, 1) + 1
    near_y = jnp.minimum(iy, 1) + jnp.minimum(ny - 1 - iy, 1) + 1
    pl.semaphore_wait(barrier, near_x * near_y - 1)

    def store(f, x, v):
        fld[f, x] = v.astype(BF16).reshape(edge, rows, ch)

    send(0)
    inner(0, pc_a)
    arrive(0)
    outer(0, pc_a)

    def use1(i, h, v):
        x = 2 * i + h
        pre[x] = v
        store(1, x, v * jax.nn.sigmoid(v) * live[...])

    conv(pc_a, w1, use1)
    send(1)
    inner(1, pc_b)
    arrive(1)
    outer(1, pc_b)

    def use2(i, h, v):
        x = 2 * i + h
        v = v + fld[0, x].reshape(plane, ch).astype(F32)
        s = jax.nn.sigmoid(v)
        out_ref[x] = (v * s * live[...]).astype(BF16).reshape(edge, rows, ch)
        g = cot[x].reshape(plane, ch).astype(F32) * (s * (1.0 + v * (1.0 - s))) * live[...]
        store(2, x, g)
        keep_t(i, h, g)

    conv(pc_b, w2, use2)
    send(2)
    inner(2, pc_c)
    wgrad(pc_b, gw2_ref)
    arrive(2)
    outer(2, pc_c)

    def use3(i, h, v):
        x = 2 * i + h
        g = v * slope(pre[x]) * live[...]
        store(3, x, g)
        keep_t(i, h, g)

    conv(pc_c, w2f, use3)
    send(3)
    inner(3, pc_c)
    wgrad(pc_a, gw1_ref)
    arrive(3)
    outer(3, pc_c)

    def use4(i, h, v):
        x = 2 * i + h
        g = (fld[2, x].reshape(plane, ch).astype(F32) + v) * live[...]
        gin_ref[x] = g.astype(BF16).reshape(edge, rows, ch)

    conv(pc_c, w1f, use4)
    for f in range(4):
        drain(f)


def selection(nb, edge, slots):
    zero = jnp.arange(slots, dtype=jnp.int32)[:, None]
    full = jnp.concatenate([nb[:, :13], zero, nb[:, 13:]], axis=1).reshape(slots, 9, 3)
    full = jnp.transpose(full, (1, 2, 0))
    z = jnp.arange(edge)
    src = z[None, :] + jnp.arange(3)[:, None] - 1
    dz = jnp.where(src < 0, 0, jnp.where(src >= edge, 2, 1))
    pick = (dz[:, :, None] == jnp.arange(3)).astype(jnp.int32)
    target = jnp.sum(pick[None, :, None, :, :] * jnp.transpose(full, (0, 2, 1))[:, None, :, None, :], axis=-1)
    hit = (target[..., None, None] == jnp.arange(slots)[:, None]) & (
        (src % edge)[None, :, None, :, None, None] == z[None, :]
    )
    return hit.astype(BF16).reshape(9, 3 * slots * edge, slots * edge)


def flipped_weight(weight):
    return jnp.transpose(weight[::-1], (0, 2, 1))


def shards(nx, ny, nd, features, cotangent, first_weight, second_weight, neighbours, counts):
    _, edge, _, slots, _, ch = features.shape
    rows = slots * edge
    plane = edge * rows
    flat = (edge, edge, rows, ch)
    scale = float(nx * ny * nd * slots * edge**3) ** -0.5
    sel = selection(neighbours[0, 0, 0], edge, slots)
    ok = (jnp.arange(slots, dtype=jnp.int32) < counts[0, 0, 0]).astype(F32)
    live = jnp.broadcast_to(ok[None, :, None, None], (edge, slots, edge, ch)).reshape(plane, ch)
    wshape = (3, 9 * ch, ch)
    vmem = pl.BlockSpec(memory_space=pltpu.VMEM)
    gshape = jax.ShapeDtypeStruct((3, 3, ch, 3 * ch), F32)
    fshape = jax.ShapeDtypeStruct(flat, BF16)
    out, gin, g1, g2 = pl.pallas_call(
        functools.partial(kernel, nx, ny),
        out_shape=[fshape, fshape, gshape, gshape],
        in_specs=[vmem] * 8,
        out_specs=[vmem] * 4,
        scratch_shapes=[
            pltpu.VMEM((4,) + flat, BF16),
            pltpu.VMEM((4, 2, edge, rows, ch), BF16),
            pltpu.VMEM((4, 2, edge, rows, ch), BF16),
            pltpu.VMEM((4, 4, rows, ch), BF16),
            pltpu.VMEM((edge + 2, edge, rows, 9 * ch), BF16),
            pltpu.VMEM((edge + 2, edge, rows, 9 * ch), BF16),
            pltpu.VMEM((edge + 2, edge, rows, 9 * ch), BF16),
            pltpu.VMEM((edge, plane, ch), F32),
            pltpu.VMEM((2 * ch, edge // 2 * plane), BF16),
            pltpu.SemaphoreType.DMA((4, len(DIRS))),
            pltpu.SemaphoreType.DMA((4, len(DIRS))),
        ],
        compiler_params=pltpu.CompilerParams(
            collective_id=0, has_side_effects=True, vmem_limit_bytes=60 * 1024 * 1024
        ),
    )(
        features.reshape(flat),
        cotangent.reshape(flat),
        first_weight.reshape(wshape),
        second_weight.reshape(wshape),
        flipped_weight(first_weight).reshape(wshape),
        flipped_weight(second_weight).reshape(wshape),
        sel,
        live,
    )
    g1, g2 = lax.psum((g1, g2), ("sx", "sy", "dp"))

    def finish(g):
        g = g.reshape(9, ch, 3, ch)
        return jnp.transpose(g, (0, 2, 3, 1)).reshape(27, ch, ch) * scale

    return out.reshape(features.shape), gin.reshape(features.shape), finish(g1), finish(g2)


def solution(mesh):
    field = P("dp", "sx", "sy", None, None, None)
    return jax.shard_map(
        functools.partial(shards, mesh.shape["sx"], mesh.shape["sy"], mesh.shape["dp"]),
        mesh=mesh,
        in_specs=(field, field, P(), P(), P("dp", "sx", "sy", None, None), P("dp", "sx", "sy")),
        out_specs=(field, field, P(), P()),
        check_vma=False,
    )
```

time: 508 us -> 214 us (0.42)
  local copies, waits for them, and re-layouts: 213 us -> 12.1 us
  other arithmetic: 96.7 us -> 3.33 us
  waiting for transfers between devices: 72.4 us -> 140 us
  matrix products: 52.4 us -> 0 us
  starting transfers between devices: 51 us -> 0.04 us
  Pallas kernels: 0 us -> 42.9 us
    unnamed x253 -> x10, local copies, waits for them, and re-layouts: 97.8 us -> 1.61 us
    gather x104 -> x0, local copies, waits for them, and re-layouts: 70.7 us -> none  [padded_blocks(): slab_piece = jnp.take(region, jnp.maximum(target, 0), axis=2) * valid]
    psum x1, waiting for transfers between devices: 72.3 us -> 140 us  [shards(): g1, g2 = lax.psum((g1, g2), ('sx', 'sy', 'dp'))]
    dot_general x6 -> x0, matrix products: 52.4 us -> none  [the longest x4 35.9 us: convolve(): jnp.dot(columns, matrix, preferred_element_type=jnp.float32).reshape(shape)]
    ppermute x16 -> x0, starting transfers between devices: 50.9 us -> none  [the longest x8 40.4 us: with_halo(): lax.ppermute(tail, axis, [(i, (i + 1) % count) for i in range(ends)])]
    pallas_call x0 -> x1, Pallas kernels: none -> 42.9 us  [shards(): pl.pallas_call(functools.partial(kernel, nx, ny), out_shape=[fshape, fsha...]
    dot_general x2 -> x0, local copies, waits for them, and re-layouts: 36.7 us -> none  [weight_partial(): lax.dot_general(columns, grads.reshape(-1, channels), (((0,), (0,)), ((),...]
    concatenate x12 -> x1, other arithmetic: 28.3 us -> 0.08 us  [selection(): jnp.concatenate([nb[:, :13], zero, nb[:, 13:]], axis=1).reshape(slots, 9, 3)]
  transfers between devices with their start and end apart: 17 -> 1, of which waited for: 1 -> 1; matrix products, arithmetic and copies ran while one was open for 36% -> 0% of each run, Pallas kernels for 0% -> 0%
where the time goes in v1:
time: 214 us; the launch traced here: 213 us
  waiting for transfers between devices  140 us (65%)
  Pallas kernels  42.9 us (20%)
  between operations  14.9 us (7%)
  local copies, waits for them, and re-layouts  12.1 us (6%)
  other arithmetic  3.33 us (2%)
    psum x1, waiting for transfers between devices, shards(): g1, g2 = lax.psum((g1, g2), ('sx', 'sy', 'dp'))  140 us
    pallas_call x1, Pallas kernels, shards(): pl.pallas_call(functools.partial(kernel, nx, ny), out_shape=[fshape, fsha...  42.9 us
  transfers between devices with their start and end apart: 1, of which 1 were waited for; matrix products, arithmetic and copies ran while one was open for 0% of the time, Pallas kernels for 0%

profile of v1, /device:TPU:0, one launch (start us, length us, event | category | flops | bytes accessed | tf_op | source)
XLA Modules:
  0.0 213.4 jit_solution(16924070015999329545)
XLA Ops:
  7.2 0.0 copy-start
  7.2 0.0 all-reduce.3.cloned.1.call-start
  8.0 0.8 fusion.3
  8.8 0.1 broadcast_in_dim.15
  8.9 0.1 broadcast_in_dim.16
  9.0 0.1 pad_add_fusion
  9.1 0.1 reshape.125
  9.2 0.1 copy.24
  9.3 0.1 multiply_reduce_fusion
  9.4 0.1 copy.25
  9.5 0.1 iota_compare_fusion
  9.6 0.1 and.36
  9.8 0.1 copy.26
  9.9 0.3 and.32
  10.2 0.6 and.33
  10.8 0.3 copy.27
  11.0 0.0 copy-start.1
  11.0 0.1 reverse_bitcast_fusion.1
  11.1 1.6 copy.22
  12.8 0.0 copy-done.1
  12.8 0.1 reverse_bitcast_fusion
  12.9 1.6 copy.23
  14.5 0.7 and_convert_fusion.sel
  15.2 0.8 broadcast_in_dim.17.live
  16.0 42.9 %shard_map.93 = (bf16[8,8,32,128]{3,2,1,0:T(8,128)(2,1)}, bf16[8,8,32,128]{3,2,1,0:T(8,128)(2,1)}, f32[3,3,128,384]{3,2,1,0:T(8,128)}, f32[3,3,128,384]{3,2,1,0:T(8,128)}) custom-call(bf16[8,8,32,128]{3,2,1,0:T(8,128)(2,1)} %bitcast.36, bf16[8,8,32,128]{3,2,1,0:T(8,128)(2,1)} %bitcast.37, bf16[3,1152,128]{2,1,0:T(8,128)(2,1)} %bitcast.30, ...), custom_call_target="tpu_custom_call" | custom-call | tf_op jit(solution)/shard_map/pallas_call | solution.py:311
  58.9 0.0 all-reduce.3.cloned.1.call-update
  59.0 140.1 %all-reduce.3.cloned.1.call-done = (f32[3,3,128,384]{3,2,1,0:T(8,128)}, f32[3,3,128,384]{3,2,1,0:T(8,128)}) async-done(((f32[3,3,128,384]{3,2,1,0:T(8,128)}, f32[3,3,128,384]{3,2,1,0:T(8,128)}), (f32[3,3,128,384]{3,2,1,0:T(8,128)}, f32[3,3,128,384]{3,2,1,0:T(8,128)})) %all-reduce.3.cloned.1.call-update) | async-done | bytes 3538960 | tf_op jit(solution)/shard_map/psum | solution.py:342
  199.0 2.3 %broadcast_multiply_fusion = (f32[3,3,128,384]{3,2,1,0:T(8,128)S(1)}, f32[3,3,128,384]{3,2,1,0:T(8,128)S(1)}) fusion(f32[3,3,128,384]{3,2,1,0:T(8,128)} %get-tuple-element.13, f32[3,3,128,384]{3,2,1,0:T(8,128)} %get-tuple-element.12), kind=kLoop, calls=%fused_computation | loop fusion | flops 884736 | bytes 7077888 | tf_op jit(solution)/shard_map/mul | solution.py:346
  201.4 1.8 copy.29
  203.2 1.8 copy.28
  205.0 0.8 copy.35
  205.7 0.8 copy.36
  (12 shorter events, 0.1 us)
Async XLA Ops:
  7.2 3.8 %copy-start = (bf16[27,128,128]{2,1,0:T(8,128)(2,1)S(1)}, bf16[27,128,128]{2,1,0:T(8,128)(2,1)}, u32[]{:S(2)}) copy-start(bf16[27,128,128]{2,1,0:T(8,128)(2,1)} %param.8) | copy-start | bytes 2654212
  7.2 191.9 %all-reduce.3.cloned.1.call-start = ((), (), s32[]{:S(2)}) async-start(), calls=%async_computation | async-start | bytes 7077888 | tf_op jit(solution)/shard_map/psum | solution.py:342
  11.0 1.7 copy-start.1
  203.2 1.8 copy-start.3
  203.2 2.6 %copy-start.2 = (bf16[8,8,32,128]{3,2,1,0:T(8,128)(2,1)S(1)}, bf16[8,8,32,128]{3,2,1,0:T(8,128)(2,1)}, u32[]{:S(2)}) copy-start(bf16[8,8,32,128]{3,2,1,0:T(8,128)(2,1)} %get-tuple-element.9) | copy-start | bytes 1572868
Sparse Core Ops, SparseCore 0:
  59.1 139.9 all-reduce.2

commit v2 on v1

--- a/solution.py
+++ b/solution.py
@@ -10,6 +10,7 @@
 DIRS = [(dx, dy) for dx in (-1, 0, 1) for dy in (-1, 0, 1) if (dx, dy) != (0, 0)]
 F32 = jnp.float32
 BF16 = jnp.bfloat16
+UNIT = 16
 
 
 def slope(v):
@@ -20,6 +21,7 @@
 def kernel(
     nx,
     ny,
+    nd,
     feat,
     cot,
     w1,
@@ -43,6 +45,19 @@
     gt,
     send_sem,
     recv_sem,
+    gb,
+    dx_buf,
+    hs,
+    rb,
+    fin,
+    pair_send,
+    pair_recv,
+    rs_send,
+    rs_recv,
+    ag_send,
+    ag_recv,
+    fw_send,
+    fw_recv,
 ):
     edge = feat.shape[0]
     rows = feat.shape[2]
@@ -169,10 +184,17 @@
     def keep_t(i, h, v):
         gt[h * ch : (h + 1) * ch, pl.ds(pl.multiple_of(i * plane, plane), plane)] = v.T.astype(BF16)
 
-    def wgrad(pc, gw):
+    def tap_out(g, a, b, v):
+        per = ch // UNIT
+        for c in range(3):
+            t = v[:, c * ch : (c + 1) * ch].T.astype(BF16).reshape(per, UNIT, ch)
+            gb[g, pl.ds(((a * 3 + b) * 3 + c) * per, per)] = t
+
+    def wgrad(pc, g):
         def body(b, carry):
+            lanes = pl.ds(pl.multiple_of(b * (3 * ch), 3 * ch), 3 * ch)
+            part = None
             for p in range(4):
-                lanes = pl.ds(pl.multiple_of(b * (3 * ch), 3 * ch), 3 * ch)
                 acc = None
                 for i in range(pairs):
                     rhs = pc[2 * i + p, :, :, lanes].reshape(plane, 3 * ch)
@@ -183,16 +205,119 @@
                         lhs = lhs[ch:]
                     t = jnp.dot(lhs, rhs, preferred_element_type=F32)
                     acc = t if acc is None else acc + t
-                if p == 0:
-                    gw[0, b] = acc
-                elif p == 3:
-                    gw[2, b] = gw[2, b] + acc
-                else:
-                    gw[p - 1, b] = gw[p - 1, b] + acc[ch:]
-                    gw[p, b] = acc[:ch]
+                if p == 3:
+                    tap_out(g, 2, b, part + acc)
+                elif p > 0:
+                    tap_out(g, p - 1, b, part + acc[ch:])
+                if p < 3:
+                    part = acc[:ch]
             return carry
 
         lax.fori_loop(0, 3, body, 0)
+
+    n = nx * ny
+    units = gb.shape[1]
+    half = units // nd
+    q = half // n
+    core = lax.axis_index("dp")
+    me = ix * ny + iy
+    mesh_id = pl.DeviceIdType.MESH
+
+    def group(p):
+        return {"sx": p // ny, "sy": lax.rem(p, ny)}
+
+    def pair_desc(g):
+        return pltpu.make_async_remote_copy(
+            src_ref=gb.at[g, pl.ds((1 - core) * half, half)],
+            dst_ref=dx_buf.at[g],
+            send_sem=pair_send.at[g],
+            recv_sem=pair_recv.at[g],
+            device_id={"dp": 1 - core},
+            device_id_type=mesh_id,
+        )
+
+    def rs_desc(g, o):
+        p = lax.rem(me + o, n)
+        return pltpu.make_async_remote_copy(
+            src_ref=hs.at[g, pl.ds(p * q, q)],
+            dst_ref=rb.at[g, o],
+            send_sem=rs_send.at[g, o],
+            recv_sem=rs_recv.at[g, o],
+            device_id=group(p),
+            device_id_type=mesh_id,
+        )
+
+    def ag_desc(g, o, owner):
+        here = pl.ds(core * half + owner * q, q)
+        return pltpu.make_async_remote_copy(
+            src_ref=fin.at[g, here],
+            dst_ref=fin.at[g, here],
+            send_sem=ag_send.at[g, o],
+            recv_sem=ag_recv.at[g, o],
+            device_id=group(lax.rem(me + o, n)),
+            device_id_type=mesh_id,
+        )
+
+    def fw_desc(g, o, side):
+        here = pl.ds(side * half + lax.rem(me + n - o, n) * q, q)
+        return pltpu.make_async_remote_copy(
+            src_ref=fin.at[g, here],
+            dst_ref=fin.at[g, here],
+            send_sem=fw_send.at[g, o],
+            recv_sem=fw_recv.at[g, o],
+            device_id={"dp": 1 - core},
+            device_id_type=mesh_id,
+        )
+
+    def each(lo, hi, fn):
+        def body(o, carry):
+            fn(o)
+            return carry
+
+        lax.fori_loop(lo, hi, body, 0)
+
+    def scatter(g):
+        pair_desc(g).wait_recv()
+
+        def one(o):
+            p = lax.rem(me + o, n)
+            mine = gb[g, pl.ds(core * half + p * q, q)].astype(F32)
+            hs[g, pl.ds(p * q, q)] = (mine + dx_buf[g, pl.ds(p * q, q)].astype(F32)).astype(BF16)
+
+        each(0, n, one)
+        each(1, n, lambda o: rs_desc(g, o).start())
+
+    def gather(g):
+        each(1, n, lambda o: rs_desc(g, o).wait_recv())
+
+        def add(o, acc):
+            return acc + rb[g, o].astype(F32)
+
+        total = lax.fori_loop(1, n, add, hs[g, pl.ds(me * q, q)].astype(F32))
+        fin[g, pl.ds(core * half + me * q, q)] = total.astype(BF16)
+        each(1, n, lambda o: ag_desc(g, o, me).start())
+        fw_desc(g, 0, core).start()
+
+    def forward(g):
+        def one(o):
+            ag_desc(g, o, lax.rem(me + n - o, n)).wait_recv()
+            fw_desc(g, o, core).start()
+
+        each(1, n, one)
+
+    def finish(g, ref):
+        each(0, n, lambda o: fw_desc(g, o, 1 - core).wait_recv())
+        ref[...] = fin[g]
+
+    def drain_sums(g):
+        pair_desc(g).wait_send()
+
+        def one(o):
+            rs_desc(g, o).wait_send()
+            ag_desc(g, o, me).wait_send()
+
+        each(1, n, one)
+        each(0, n, lambda o: fw_desc(g, o, core).wait_send())
 
     for dx, dy in DIRS:
         @pl.when(jnp.logical_not(there(dx, dy)))
@@ -202,10 +327,19 @@
                 r[...] = jnp.zeros(r.shape, BF16)
 
     barrier = pltpu.get_barrier_semaphore()
-    for dx, dy in DIRS:
-        @pl.when(there(dx, dy))
-        def _(dx=dx, dy=dy):
-            pl.semaphore_signal(barrier, inc=1, device_id=peer(dx, dy), device_id_type=pl.DeviceIdType.MESH)
+    each(
+        1,
+        n,
+        lambda o: pl.semaphore_signal(
+            barrier, inc=1, device_id=group(lax.rem(me + o, n)), device_id_type=mesh_id
+        ),
+    )
+    pl.semaphore_signal(barrier, inc=1, device_id={"dp": 1 - core}, device_id_type=mesh_id)
+
+    spare = units - 27 * (ch // UNIT)
+    if spare:
+        for g in range(2):
+            gb[g, units - spare :] = jnp.zeros((spare, UNIT, ch), BF16)
 
     def mask_in(x, carry):
         v = feat[x].astype(F32).reshape(plane, ch) * live[...]
@@ -214,9 +348,7 @@
 
     lax.fori_loop(0, edge, mask_in, 0)
 
-    near_x = jnp.minimum(ix, 1) + jnp.minimum(nx - 1 - ix, 1) + 1
-    near_y = jnp.minimum(iy, 1) + jnp.minimum(ny - 1 - iy, 1) + 1
-    pl.semaphore_wait(barrier, near_x * near_y - 1)
+    pl.semaphore_wait(barrier, n)
 
     def store(f, x, v):
         fld[f, x] = v.astype(BF16).reshape(edge, rows, ch)
@@ -249,9 +381,11 @@
     conv(pc_b, w2, use2)
     send(2)
     inner(2, pc_c)
-    wgrad(pc_b, gw2_ref)
+    wgrad(pc_b, 0)
+    pair_desc(0).start()
     arrive(2)
     outer(2, pc_c)
+    scatter(0)
 
     def use3(i, h, v):
         x = 2 * i + h
@@ -262,7 +396,10 @@
     conv(pc_c, w2f, use3)
     send(3)
     inner(3, pc_c)
-    wgrad(pc_a, gw1_ref)
+    wgrad(pc_a, 1)
+    pair_desc(1).start()
+    gather(0)
+    scatter(1)
     arrive(3)
     outer(3, pc_c)
 
@@ -272,8 +409,15 @@
         gin_ref[x] = g.astype(BF16).reshape(edge, rows, ch)
 
     conv(pc_c, w1f, use4)
+    gather(1)
+    forward(0)
+    forward(1)
+    finish(0, gw2_ref)
+    finish(1, gw1_ref)
     for f in range(4):
         drain(f)
+    drain_sums(0)
+    drain_sums(1)
 
 
 def selection(nb, edge, slots):
@@ -306,10 +450,13 @@
     live = jnp.broadcast_to(ok[None, :, None, None], (edge, slots, edge, ch)).reshape(plane, ch)
     wshape = (3, 9 * ch, ch)
     vmem = pl.BlockSpec(memory_space=pltpu.VMEM)
-    gshape = jax.ShapeDtypeStruct((3, 3, ch, 3 * ch), F32)
+    n = nx * ny
+    q = -(-27 * ch // (UNIT * n * nd))
+    units = q * n * nd
+    gshape = jax.ShapeDtypeStruct((units, UNIT, ch), BF16)
     fshape = jax.ShapeDtypeStruct(flat, BF16)
     out, gin, g1, g2 = pl.pallas_call(
-        functools.partial(kernel, nx, ny),
+        functools.partial(kernel, nx, ny, nd),
         out_shape=[fshape, fshape, gshape, gshape],
         in_specs=[vmem] * 8,
         out_specs=[vmem] * 4,
@@ -325,7 +472,14 @@
             pltpu.VMEM((2 * ch, edge // 2 * plane), BF16),
             pltpu.SemaphoreType.DMA((4, len(DIRS))),
             pltpu.SemaphoreType.DMA((4, len(DIRS))),
-        ],
+            pltpu.VMEM((2, units, UNIT, ch), BF16),
+            pltpu.VMEM((2, units // nd, UNIT, ch), BF16),
+            pltpu.VMEM((2, units // nd, UNIT, ch), BF16),
+            pltpu.VMEM((2, n, q, UNIT, ch), BF16),
+            pltpu.VMEM((2, units, UNIT, ch), BF16),
+        ]
+        + [pltpu.SemaphoreType.DMA((2,))] * 2
+        + [pltpu.SemaphoreType.DMA((2, n))] * 6,
         compiler_params=pltpu.CompilerParams(
             collective_id=0, has_side_effects=True, vmem_limit_bytes=60 * 1024 * 1024
         ),
@@ -339,11 +493,9 @@
         sel,
         live,
     )
-    g1, g2 = lax.psum((g1, g2), ("sx", "sy", "dp"))
-
     def finish(g):
-        g = g.reshape(9, ch, 3, ch)
-        return jnp.transpose(g, (0, 2, 3, 1)).reshape(27, ch, ch) * scale
+        g = g.reshape(-1, ch)[: 27 * ch]
+        return g.reshape(27, ch, ch).astype(F32) * scale
 
     return out.reshape(features.shape), gin.reshape(features.shape), finish(g1), finish(g2)
 

time: 214 us -> 95.3 us (0.45)
  the two profiles are of different devices: /device:TPU:0 before, /device:TPU:29 now
where the time goes in v2:
time: 95.3 us; the launch traced here: 95.1 us
  Pallas kernels  80.5 us (84%)
  local copies, waits for them, and re-layouts  8.52 us (9%)
  other arithmetic  4.61 us (5%)
  between operations  1.5 us (2%)
    pallas_call x1, Pallas kernels, shards(): pl.pallas_call(functools.partial(kernel, nx, ny, nd), out_shape=[fshape,...  80.5 us
    mul x1, other arithmetic, finish(): return g.reshape(27, ch, ch).astype(F32) * scale  3.59 us
    transpose x4, local copies, waits for them, and re-layouts, flipped_weight(): return jnp.transpose(weight[::-1], (0, 2, 1))  3.44 us

profile of v2, /device:TPU:29, one launch (start us, length us, event | category | flops | bytes accessed | tf_op | source)
XLA Modules:
  0.0 95.1 jit_solution(12063732389650067315)
XLA Ops:
  0.6 0.0 copy-start
  1.4 0.8 fusion.3
  2.3 0.1 pad_add_fusion
  2.4 0.1 broadcast_in_dim.15
  2.4 0.1 broadcast_in_dim.16
  2.5 0.1 reshape.127
  2.6 0.1 copy.20
  2.7 0.1 multiply_reduce_fusion
  2.8 0.1 copy.21
  3.0 0.1 iota_compare_fusion
  3.1 0.1 and.36
  3.2 0.1 copy.22
  3.3 0.8 broadcast_in_dim.17.live
  4.1 0.3 and.32
  4.3 0.6 and.33
  4.9 0.3 copy.23
  5.2 0.8 and_convert_fusion.sel
  6.0 0.0 copy-done
  6.0 0.0 copy-start.1
  6.0 0.1 reverse_bitcast_fusion.1
  6.0 1.6 %copy.18 = bf16[27,128,128]{2,1,0:T(8,128)(2,1)} copy(bf16[27,128,128]{1,2,0:T(8,128)(2,1)S(1)} %reverse_bitcast_fusion.1) | data formatting | bytes 1769472 | tf_op jit(solution)/shard_map/transpose | solution.py:439
  7.7 0.0 copy-done.1
  7.7 0.1 reverse_bitcast_fusion
  7.8 1.6 %copy.19 = bf16[27,128,128]{2,1,0:T(8,128)(2,1)} copy(bf16[27,128,128]{1,2,0:T(8,128)(2,1)S(1)} %reverse_bitcast_fusion) | data formatting | bytes 1769472 | tf_op jit(solution)/shard_map/transpose | solution.py:439
  9.4 80.5 %shard_map.93 = (bf16[8,8,32,128]{3,2,1,0:T(8,128)(2,1)}, bf16[8,8,32,128]{3,2,1,0:T(8,128)(2,1)}, bf16[224,16,128]{2,1,0:T(8,128)(2,1)}, bf16[224,16,128]{2,1,0:T(8,128)(2,1)}) custom-call(bf16[8,8,32,128]{3,2,1,0:T(8,128)(2,1)} %bitcast.28, bf16[8,8,32,128]{3,2,1,0:T(8,128)(2,1)} %bitcast.29, bf16[3,1152,128]{2,1,0:T(8,128)(2,1)} %bitcast.22, ...), custom_call_target="tpu_custom_call" | custom-call | tf_op jit(solution)/shard_map/pallas_call | solution.py:458
  89.9 0.0 copy-start.3
  89.9 0.0 copy-start.2
  90.0 3.6 %convert_multiply_fusion = (f32[216,16,128]{2,1,0:T(8,128)}, f32[216,16,128]{2,1,0:T(8,128)}) fusion(bf16[224,16,128]{2,1,0:T(8,128)(2,1)} %get-tuple-element.11, bf16[224,16,128]{2,1,0:T(8,128)(2,1)} %get-tuple-element.10), kind=kLoop, calls=%fused_computation | loop fusion | flops 1769472 | bytes 5308416 | tf_op jit(solution)/shard_map/mul | solution.py:498
  93.5 0.0 copy-done.3
  93.5 0.8 copy.27
  94.3 0.0 copy-done.2
  94.3 0.8 copy.28
  (7 shorter events, 0.1 us)
Async XLA Ops:
  0.6 5.3 %copy-start = (bf16[27,128,128]{2,1,0:T(8,128)(2,1)S(1)}, bf16[27,128,128]{2,1,0:T(8,128)(2,1)}, u32[]{:S(2)}) copy-start(bf16[27,128,128]{2,1,0:T(8,128)(2,1)} %param.8) | copy-start | bytes 2654212
  6.0 1.7 %copy-start.1 = (bf16[27,128,128]{2,1,0:T(8,128)(2,1)S(1)}, bf16[27,128,128]{2,1,0:T(8,128)(2,1)}, u32[]{:S(2)}) copy-start(bf16[27,128,128]{2,1,0:T(8,128)(2,1)} %param.9) | copy-start | bytes 2654212
  89.9 3.6 %copy-start.3 = (bf16[8,8,32,128]{3,2,1,0:T(8,128)(2,1)S(1)}, bf16[8,8,32,128]{3,2,1,0:T(8,128)(2,1)}, u32[]{:S(2)}) copy-start(bf16[8,8,32,128]{3,2,1,0:T(8,128)(2,1)} %get-tuple-element.8) | copy-start | bytes 1572868
  89.9 4.4 %copy-start.2 = (bf16[8,8,32,128]{3,2,1,0:T(8,128)(2,1)S(1)}, bf16[8,8,32,128]{3,2,1,0:T(8,128)(2,1)}, u32[]{:S(2)}) copy-start(bf16[8,8,32,128]{3,2,1,0:T(8,128)(2,1)} %get-tuple-element.9) | copy-start | bytes 1572868

commit v3 on v2

--- a/solution.py
+++ b/solution.py
@@ -26,10 +26,8 @@
     cot,
     w1,
     w2,
-    w1f,
-    w2f,
-    sel,
-    live,
+    nb,
+    count,
     out_ref,
     gin_ref,
     gw1_ref,
@@ -45,6 +43,10 @@
     gt,
     send_sem,
     recv_sem,
+    w1f,
+    w2f,
+    sel,
+    live,
     gb,
     dx_buf,
     hs,
@@ -165,8 +167,8 @@
             right = None
             for p in range(4):
                 lhs = pc[2 * i + p].reshape(plane, 9 * ch)
-                wl = w[p] if p < 3 else None
-                wr = w[p - 1] if p > 0 else None
+                wl = w[9 * p : 9 * p + 9].reshape(9 * ch, ch) if p < 3 else None
+                wr = w[9 * p - 9 : 9 * p].reshape(9 * ch, ch) if p > 0 else None
                 if wr is None:
                     left = jnp.dot(lhs, wl, preferred_element_type=F32)
                 elif wl is None:
@@ -341,6 +343,34 @@
         for g in range(2):
             gb[g, units - spare :] = jnp.zeros((spare, UNIT, ch), BF16)
 
+    slots = rows // edge
+    row = lax.broadcasted_iota(jnp.int32, (plane, ch), 0)
+    live[...] = jnp.where(lax.rem(lax.div(row, edge), slots) < count[0], 1.0, 0.0).astype(F32)
+
+    r = lax.broadcasted_iota(jnp.int32, (3 * rows, rows), 0)
+    col = lax.broadcasted_iota(jnp.int32, (3 * rows, rows), 1)
+    src = lax.rem(r, edge) + lax.div(r, rows) - 1
+    dz = jnp.where(src < 0, 0, jnp.where(src >= edge, 2, 1))
+    key = dz * slots + lax.rem(lax.div(r, edge), slots)
+    same_z = lax.rem(src + edge, edge) == lax.rem(col, edge)
+    slot = lax.div(col, edge)
+    for d in range(9):
+        target = jnp.full((3 * rows, rows), -1, jnp.int32)
+        for k in range(3):
+            way = d * 3 + k
+            for sl in range(slots):
+                name = sl if way == 13 else nb[sl, way if way < 13 else way - 1]
+                target = jnp.where(key == k * slots + sl, name, target)
+        hit = jnp.logical_and(same_z, target == slot)
+        sel[d] = jnp.where(hit, 1.0, 0.0).astype(F32).astype(BF16)
+
+    def flip(w, to):
+        def body(k, carry):
+            to[k] = w[26 - k].astype(F32).T.astype(BF16)
+            return carry
+
+        lax.fori_loop(0, 27, body, 0)
+
     def mask_in(x, carry):
         v = feat[x].astype(F32).reshape(plane, ch) * live[...]
         fld[0, x] = v.astype(BF16).reshape(edge, rows, ch)
@@ -355,6 +385,7 @@
 
     send(0)
     inner(0, pc_a)
+    flip(w2, w2f)
     arrive(0)
     outer(0, pc_a)
 
@@ -366,6 +397,7 @@
     conv(pc_a, w1, use1)
     send(1)
     inner(1, pc_b)
+    flip(w1, w1f)
     arrive(1)
     outer(1, pc_b)
 
@@ -395,13 +427,14 @@
 
     conv(pc_c, w2f, use3)
     send(3)
-    inner(3, pc_c)
+    gather(0)
     wgrad(pc_a, 1)
     pair_desc(1).start()
-    gather(0)
+    inner(3, pc_c)
     scatter(1)
     arrive(3)
     outer(3, pc_c)
+    forward(0)
 
     def use4(i, h, v):
         x = 2 * i + h
@@ -410,7 +443,6 @@
 
     conv(pc_c, w1f, use4)
     gather(1)
-    forward(0)
     forward(1)
     finish(0, gw2_ref)
     finish(1, gw1_ref)
@@ -420,36 +452,14 @@
     drain_sums(1)
 
 
-def selection(nb, edge, slots):
-    zero = jnp.arange(slots, dtype=jnp.int32)[:, None]
-    full = jnp.concatenate([nb[:, :13], zero, nb[:, 13:]], axis=1).reshape(slots, 9, 3)
-    full = jnp.transpose(full, (1, 2, 0))
-    z = jnp.arange(edge)
-    src = z[None, :] + jnp.arange(3)[:, None] - 1
-    dz = jnp.where(src < 0, 0, jnp.where(src >= edge, 2, 1))
-    pick = (dz[:, :, None] == jnp.arange(3)).astype(jnp.int32)
-    target = jnp.sum(pick[None, :, None, :, :] * jnp.transpose(full, (0, 2, 1))[:, None, :, None, :], axis=-1)
-    hit = (target[..., None, None] == jnp.arange(slots)[:, None]) & (
-        (src % edge)[None, :, None, :, None, None] == z[None, :]
-    )
-    return hit.astype(BF16).reshape(9, 3 * slots * edge, slots * edge)
-
-
-def flipped_weight(weight):
-    return jnp.transpose(weight[::-1], (0, 2, 1))
-
-
 def shards(nx, ny, nd, features, cotangent, first_weight, second_weight, neighbours, counts):
     _, edge, _, slots, _, ch = features.shape
     rows = slots * edge
     plane = edge * rows
     flat = (edge, edge, rows, ch)
     scale = float(nx * ny * nd * slots * edge**3) ** -0.5
-    sel = selection(neighbours[0, 0, 0], edge, slots)
-    ok = (jnp.arange(slots, dtype=jnp.int32) < counts[0, 0, 0]).astype(F32)
-    live = jnp.broadcast_to(ok[None, :, None, None], (edge, slots, edge, ch)).reshape(plane, ch)
-    wshape = (3, 9 * ch, ch)
     vmem = pl.BlockSpec(memory_space=pltpu.VMEM)
+    smem = pl.BlockSpec(memory_space=pltpu.SMEM)
     n = nx * ny
     q = -(-27 * ch // (UNIT * n * nd))
     units = q * n * nd
@@ -458,7 +468,7 @@
     out, gin, g1, g2 = pl.pallas_call(
         functools.partial(kernel, nx, ny, nd),
         out_shape=[fshape, fshape, gshape, gshape],
-        in_specs=[vmem] * 8,
+        in_specs=[vmem] * 4 + [smem] * 2,
         out_specs=[vmem] * 4,
         scratch_shapes=[
             pltpu.VMEM((4,) + flat, BF16),
@@ -472,6 +482,10 @@
             pltpu.VMEM((2 * ch, edge // 2 * plane), BF16),
             pltpu.SemaphoreType.DMA((4, len(DIRS))),
             pltpu.SemaphoreType.DMA((4, len(DIRS))),
+            pltpu.VMEM((27, ch, ch), BF16),
+            pltpu.VMEM((27, ch, ch), BF16),
+            pltpu.VMEM((9, 3 * rows, rows), BF16),
+            pltpu.VMEM((plane, ch), F32),
             pltpu.VMEM((2, units, UNIT, ch), BF16),
             pltpu.VMEM((2, units // nd, UNIT, ch), BF16),
             pltpu.VMEM((2, units // nd, UNIT, ch), BF16),
@@ -486,12 +500,10 @@
     )(
         features.reshape(flat),
         cotangent.reshape(flat),
-        first_weight.reshape(wshape),
-        second_weight.reshape(wshape),
-        flipped_weight(first_weight).reshape(wshape),
-        flipped_weight(second_weight).reshape(wshape),
-        sel,
-        live,
+        first_weight,
+        second_weight,
+        neighbours[0, 0, 0],
+        counts.reshape(1),
     )
     def finish(g):
         g = g.reshape(-1, ch)[: 27 * ch]

time: 95.3 us -> 87 us (0.913)
  local copies, waits for them, and re-layouts: 8.52 us -> 1.59 us
  other arithmetic: 4.61 us -> 3.59 us
    transpose x4 -> x0, local copies, waits for them, and re-layouts: 3.44 us -> none  [flipped_weight(): return jnp.transpose(weight[::-1], (0, 2, 1))]
    and x6 -> x0, local copies, waits for them, and re-layouts: 1.38 us -> none  [selection(): (target[..., None, None] == jnp.arange(slots)[:, None]) & ((src % edge)[N...]
where the time goes in v3:
time: 87 us; the launch traced here: 86.9 us
  Pallas kernels  80.4 us (92%)
  other arithmetic  3.59 us (4%)
  local copies, waits for them, and re-layouts  1.59 us (2%)
  between operations  1.3 us (1%)
    pallas_call x1, Pallas kernels, shards(): pl.pallas_call(functools.partial(kernel, nx, ny, nd), out_shape=[fshape,...  80.4 us
    mul x1, other arithmetic, finish(): return g.reshape(27, ch, ch).astype(F32) * scale  3.59 us

profile of v3, /device:TPU:29, one launch (start us, length us, event | category | flops | bytes accessed | tf_op | source)
XLA Modules:
  0.0 86.9 jit_solution(14574239925856370515)
XLA Ops:
  1.3 80.4 %shard_map.93 = (bf16[8,8,32,128]{3,2,1,0:T(8,128)(2,1)}, bf16[8,8,32,128]{3,2,1,0:T(8,128)(2,1)}, bf16[224,16,128]{2,1,0:T(8,128)(2,1)}, bf16[224,16,128]{2,1,0:T(8,128)(2,1)}) custom-call(bf16[8,8,32,128]{3,2,1,0:T(8,128)(2,1)} %bitcast.13, bf16[8,8,32,128]{3,2,1,0:T(8,128)(2,1)} %bitcast.14, bf16[27,128,128]{2,1,0:T(8,128)(2,1)} %w1.1, ...), custom_call_target="tpu_custom_call" | custom-call | tf_op jit(solution)/shard_map/pallas_call | solution.py:468
  81.7 0.0 copy-start.1
  81.7 0.0 copy-start
  81.7 3.6 %convert_multiply_fusion = (f32[216,16,128]{2,1,0:T(8,128)}, f32[216,16,128]{2,1,0:T(8,128)}) fusion(bf16[224,16,128]{2,1,0:T(8,128)(2,1)} %get-tuple-element.11, bf16[224,16,128]{2,1,0:T(8,128)(2,1)} %get-tuple-element.10), kind=kLoop, calls=%fused_computation | loop fusion | flops 1769472 | bytes 5308416 | tf_op jit(solution)/shard_map/mul | solution.py:510
  85.3 0.0 copy-done.1
  85.3 0.8 copy.13
  86.1 0.0 copy-done
  86.1 0.8 copy.14
Async XLA Ops:
  81.7 3.6 %copy-start.1 = (bf16[8,8,32,128]{3,2,1,0:T(8,128)(2,1)S(1)}, bf16[8,8,32,128]{3,2,1,0:T(8,128)(2,1)}, u32[]{:S(2)}) copy-start(bf16[8,8,32,128]{3,2,1,0:T(8,128)(2,1)} %get-tuple-element.8) | copy-start | bytes 1572868
  81.7 4.4 %copy-start = (bf16[8,8,32,128]{3,2,1,0:T(8,128)(2,1)S(1)}, bf16[8,8,32,128]{3,2,1,0:T(8,128)(2,1)}, u32[]{:S(2)}) copy-start(bf16[8,8,32,128]{3,2,1,0:T(8,128)(2,1)} %get-tuple-element.9) | copy-start | bytes 1572868

commit v4 on v3

--- a/solution.py
+++ b/solution.py
@@ -192,7 +192,7 @@
             t = v[:, c * ch : (c + 1) * ch].T.astype(BF16).reshape(per, UNIT, ch)
             gb[g, pl.ds(((a * 3 + b) * 3 + c) * per, per)] = t
 
-    def wgrad(pc, g):
+    def wgrad(pc, g, lo, hi):
         def body(b, carry):
             lanes = pl.ds(pl.multiple_of(b * (3 * ch), 3 * ch), 3 * ch)
             part = None
@@ -215,7 +215,7 @@
                     part = acc[:ch]
             return carry
 
-        lax.fori_loop(0, 3, body, 0)
+        lax.fori_loop(lo, hi, body, 0)
 
     n = nx * ny
     units = gb.shape[1]
@@ -286,8 +286,12 @@
             mine = gb[g, pl.ds(core * half + p * q, q)].astype(F32)
             hs[g, pl.ds(p * q, q)] = (mine + dx_buf[g, pl.ds(p * q, q)].astype(F32)).astype(BF16)
 
-        each(0, n, one)
-        each(1, n, lambda o: rs_desc(g, o).start())
+        def go(o):
+            one(o)
+            rs_desc(g, o).start()
+
+        each(1, n, go)
+        one(0)
 
     def gather(g):
         each(1, n, lambda o: rs_desc(g, o).wait_recv())
@@ -413,7 +417,7 @@
     conv(pc_b, w2, use2)
     send(2)
     inner(2, pc_c)
-    wgrad(pc_b, 0)
+    wgrad(pc_b, 0, 0, 3)
     pair_desc(0).start()
     arrive(2)
     outer(2, pc_c)
@@ -427,8 +431,9 @@
 
     conv(pc_c, w2f, use3)
     send(3)
+    wgrad(pc_a, 1, 0, 2)
     gather(0)
-    wgrad(pc_a, 1)
+    wgrad(pc_a, 1, 2, 3)
     pair_desc(1).start()
     inner(3, pc_c)
     scatter(1)
@@ -442,9 +447,9 @@
         gin_ref[x] = g.astype(BF16).reshape(edge, rows, ch)
 
     conv(pc_c, w1f, use4)
+    finish(0, gw2_ref)
     gather(1)
     forward(1)
-    finish(0, gw2_ref)
     finish(1, gw1_ref)
     for f in range(4):
         drain(f)

time: 87 us -> 86.7 us (level)
  no operation moved by 1% of the time
where the time goes in v4:
time: 86.7 us; the launch traced here: 86.5 us
  Pallas kernels  80 us (92%)
  other arithmetic  3.59 us (4%)
  local copies, waits for them, and re-layouts  1.59 us (2%)
  between operations  1.3 us (1%)
    pallas_call x1, Pallas kernels, shards(): pl.pallas_call(functools.partial(kernel, nx, ny, nd), out_shape=[fshape,...  80 us
    mul x1, other arithmetic, finish(): return g.reshape(27, ch, ch).astype(F32) * scale  3.59 us

profile of v4, /device:TPU:29, one launch (start us, length us, event | category | flops | bytes accessed | tf_op | source)
XLA Modules:
  0.0 86.5 jit_solution(16873384484820189207)
XLA Ops:
  1.3 80.0 %shard_map.93 = (bf16[8,8,32,128]{3,2,1,0:T(8,128)(2,1)}, bf16[8,8,32,128]{3,2,1,0:T(8,128)(2,1)}, bf16[224,16,128]{2,1,0:T(8,128)(2,1)}, bf16[224,16,128]{2,1,0:T(8,128)(2,1)}) custom-call(bf16[8,8,32,128]{3,2,1,0:T(8,128)(2,1)} %bitcast.13, bf16[8,8,32,128]{3,2,1,0:T(8,128)(2,1)} %bitcast.14, bf16[27,128,128]{2,1,0:T(8,128)(2,1)} %w1.1, ...), custom_call_target="tpu_custom_call" | custom-call | tf_op jit(solution)/shard_map/pallas_call | solution.py:473
  81.3 0.0 copy-start.1
  81.3 0.0 copy-start
  81.4 3.6 %convert_multiply_fusion = (f32[216,16,128]{2,1,0:T(8,128)}, f32[216,16,128]{2,1,0:T(8,128)}) fusion(bf16[224,16,128]{2,1,0:T(8,128)(2,1)} %get-tuple-element.11, bf16[224,16,128]{2,1,0:T(8,128)(2,1)} %get-tuple-element.10), kind=kLoop, calls=%fused_computation | loop fusion | flops 1769472 | bytes 5308416 | tf_op jit(solution)/shard_map/mul | solution.py:515
  84.9 0.0 copy-done.1
  84.9 0.8 copy.13
  85.7 0.0 copy-done
  85.7 0.8 copy.14
Async XLA Ops:
  81.3 3.6 %copy-start.1 = (bf16[8,8,32,128]{3,2,1,0:T(8,128)(2,1)S(1)}, bf16[8,8,32,128]{3,2,1,0:T(8,128)(2,1)}, u32[]{:S(2)}) copy-start(bf16[8,8,32,128]{3,2,1,0:T(8,128)(2,1)} %get-tuple-element.8) | copy-start | bytes 1572868
  81.3 4.4 %copy-start = (bf16[8,8,32,128]{3,2,1,0:T(8,128)(2,1)S(1)}, bf16[8,8,32,128]{3,2,1,0:T(8,128)(2,1)}, u32[]{:S(2)}) copy-start(bf16[8,8,32,128]{3,2,1,0:T(8,128)(2,1)} %get-tuple-element.9) | copy-start | bytes 1572868
